TPU v7x, 32 devices: a whole 2x2x4 slice. The times are simulated.
32 devices in a mesh: wide: 8 (over z, y), narrow: 4 (over x, core).
Axes of the slice: x: 2, y: 2, z: 4, core: 2. Of those that a mesh axis runs over, the one named last changes fastest.
Arguments:
- frames: float32 [32768, 440], P(('wide', 'narrow')), may hold values from -8 to 8
- targets: float32 [32768, 2048], P(('wide', 'narrow')), may hold values from -7 to 7
- projection: float32 [32, 440, 512], P(('wide', 'narrow')), may hold values from -0.25 to 0.25
- phases: float32 [32, 512], P(('wide', 'narrow')), may hold values from 0 to 6.283185
- block_order: int32 [32], replicated, may hold values from 0 to 31, each once
Outputs:
- residual: float32 [32768, 2048], P(('wide', 'narrow'))
- weights: float32 [2, 512, 2048], replicated
Inputs may be any that keep to these rules, and one draw needn't show every extreme that they name: `block_order`: a permutation; steps use its first 2 entries.
All inputs are finite; a program needn't handle non-finite values.
Results may differ from a plain program's by a relative error of at most 0.0003.
Values sent between devices are 32-bit elements; how exact they have to be, the bound alone decides.
No kernel may reach another device: no remote copies, remote signals or barrier semaphores. Data moves between devices by JAX's collectives and lax.ppermute only.
A program may use at most 128 MiB of HBM per device.

v0:
```python
import jax
import jax.numpy as jnp
from jax import lax
from jax.sharding import PartitionSpec as P

STEPS = 2


def from_root(value, axis, source):
    kept = jnp.where(lax.axis_index(axis) == source, value, 0).astype(value.dtype)
    return lax.psum(kept, axis)


def features_of(frames, block_proj, block_phase):
    inner = jnp.dot(
        frames, block_proj, precision=lax.Precision.HIGHEST, preferred_element_type=jnp.float32
    )
    return jnp.sqrt(2.0 / block_proj.shape[1]) * jnp.cos(inner + block_phase[None, :])


def local_product(left, right):
    return jnp.dot(
        left.T, right, precision=lax.Precision.HIGHEST, preferred_element_type=jnp.float32
    )


def solve_block(gram_sum, cross_sum):
    width = gram_sum.shape[0]
    damping = 0.1 * jnp.trace(gram_sum) / width
    factor = jnp.linalg.cholesky(gram_sum + damping * jnp.eye(width, dtype=gram_sum.dtype))
    return jax.scipy.linalg.cho_solve((factor, True), cross_sum)


def per_device(frames, targets, projection, phases, block_order):
    feature_list = []
    for step_index in range(STEPS):
        block_proj, block_phase = (
            from_root(projection, ("wide", "narrow"), block_order[step_index]),
            from_root(phases, ("wide", "narrow"), block_order[step_index]),
        )
        feature_list.append(features_of(frames, block_proj[0], block_phase[0]))
    residual = targets
    solved = []
    for step_index in range(STEPS):
        feats = feature_list[step_index]
        cross_local = local_product(feats, residual)
        gram_sum = lax.psum(local_product(feats, feats), ("wide", "narrow"))
        cross_share = lax.psum_scatter(cross_local, "narrow", scatter_dimension=1, tiled=True)
        cross_share = lax.psum(cross_share, "wide")
        weight_share = solve_block(gram_sum, cross_share)
        weights = lax.all_gather(weight_share, "narrow", axis=1, tiled=True)
        residual = residual - jnp.dot(
            feats, weights, precision=lax.Precision.HIGHEST, preferred_element_type=jnp.float32
        )
        solved.append(weights)
    return (residual, jnp.stack(solved))


def solution(mesh):
    return jax.shard_map(
        per_device,
        mesh=mesh,
        in_specs=(
            P(("wide", "narrow"), None),
            P(("wide", "narrow"), None),
            P(("wide", "narrow"), None, None),
            P(("wide", "narrow"), None),
            P(),
        ),
        out_specs=(P(("wide", "narrow"), None), P()),
        check_vma=False,
    )
```

profile of v0, /device:TPU:0, one launch (start us, length us, event | category | flops | bytes accessed | tf_op | source)
XLA Modules:
  0.0 830.9 jit_solution(9541933310264790107)
XLA Ops:
  7.2 1.4 fusion.96
  9.9 2.6 select_bitcast_fusion
  12.6 42.1 %all-reduce.1 = (f32[512]{0:T(512)S(1)}, f32[512]{0:T(512)S(1)}) all-reduce(f32[512]{0:T(512)S(1)} %bitcast.143, f32[512]{0:T(512)S(1)} %bitcast.142), channel_id=1, replica_groups=mesh['wide'=8,'narrow'=4] {'wide','narrow'}, use_global_device_ids=true, to_apply=%region_1.2 | all-reduce | flops 1024 | bytes 8192 | tf_op jit(solution)/shard_map/psum | solution.py:11
  54.7 96.0 %all-reduce.15.cloned.1.call-done = (f32[440,512]{1,0:T(8,128)}, f32[440,512]{1,0:T(8,128)}) async-done(((f32[440,512]{1,0:T(8,128)}, f32[440,512]{1,0:T(8,128)}), (f32[440,512]{1,0:T(8,128)}, f32[440,512]{1,0:T(8,128)})) %all-reduce.15.cloned.1.call-update) | async-done | bytes 1802256 | tf_op jit(solution)/shard_map/psum | solution.py:11
  150.7 11.2 %cosine_multiply_fusion.1 = f32[512,1024]{1,0:T(8,128)S(1)} fusion(f32[440,512]{1,0:T(8,128)} %get-tuple-element.40, f32[1024,440]{0,1:T(8,128)S(1)} %copy-done, f32[512]{0:T(512)S(1)} %get-tuple-element.36), kind=kOutput, calls=%fused_computation.8 | convolution fusion | flops 2769289216 | bytes 4802560 | tf_op jit(solution)/shard_map/dot_general | solution.py:15
  162.0 13.4 %fusion.97 = f32[512,512]{0,1:T(8,128)} fusion(f32[512,1024]{1,0:T(8,128)S(1)} %cosine_multiply_fusion.1), kind=kOutput, calls=%fused_computation.185 | convolution fusion | flops 3221225472 | bytes 3145728 | tf_op jit(solution)/shard_map/dot_general | solution.py:22
  175.3 10.3 %cosine_multiply_fusion = f32[512,1024]{1,0:T(8,128)S(1)} fusion(f32[440,512]{1,0:T(8,128)S(1)} %copy-done.11, f32[1024,440]{0,1:T(8,128)S(1)} %copy-done, f32[512]{0:T(512)S(1)} %get-tuple-element.37), kind=kOutput, calls=%fused_computation.7 | convolution fusion | flops 2769289216 | bytes 4802560 | tf_op jit(solution)/shard_map/dot_general | solution.py:15
  185.7 1.4 copy-done.3
  187.1 4.5 fusion.99
  191.7 18.0 %fusion.98 = f32[512,2048]{1,0:T(8,128)} fusion(f32[512,1024]{1,0:T(8,128)} %copy-done.5, f32[1024,2048]{1,0:T(8,128)} %param.9), kind=kOutput, calls=%fused_computation.186 | convolution fusion | flops 12884901888 | bytes 14680064 | tf_op jit(solution)/shard_map/dot_general | solution.py:22
  210.2 115.3 %all-reduce.13.cloned.1.call-done = (f32[512,512]{0,1:T(8,128)}, f32[512,512]{0,1:T(8,128)}) async-done(((f32[512,512]{0,1:T(8,128)}, f32[512,512]{0,1:T(8,128)}), (f32[512,512]{0,1:T(8,128)}, f32[512,512]{0,1:T(8,128)})) %all-reduce.13.cloned.1.call-update) | async-done | bytes 2097168 | tf_op jit(solution)/shard_map/psum | solution.py:47
  325.5 2.0 select_reduce_fusion
  328.1 2.0 select_reduce_fusion.1
  330.7 1.8 select_add_fusion
  332.5 1.4 copy.8
  333.9 1.5 fusion.1
  336.4 11.7 %cholesky.286 = f32[128,128]{1,0:T(8,128)S(1)} custom-call(f32[128,128]{1,0:T(8,128)S(1)} %cholesky.426), custom_call_target="Cholesky" | custom-call | tf_op jit(solution)/shard_map/jit(cholesky)/cholesky | solution.py:30
  348.2 9.8 %custom-call.29 = f32[1,128,128]{1,2,0:T(8,128)S(1)} custom-call(f32[1,128,128]{2,1,0:T(8,128)S(1)} %get-tuple-element.67), custom_call_target="InvertDiagBlocksLowerTriangular" | custom-call | tf_op jit(solution)/shard_map/jit(cholesky)/cholesky | solution.py:30
  358.1 1.2 constant_dynamic-update-slice_fusion.5
  359.3 1.3 convolution_subtract_fusion.15
  360.6 11.7 %cholesky.305 = f32[128,128]{1,0:T(8,128)S(1)} custom-call(f32[128,128]{1,0:T(8,128)S(1)} %cholesky.430), custom_call_target="Cholesky" | custom-call | tf_op jit(solution)/shard_map/jit(cholesky)/cholesky | solution.py:30
  372.4 10.0 %custom-call.30 = f32[1,128,128]{1,2,0:T(8,128)S(1)} custom-call(f32[1,128,128]{2,1,0:T(8,128)S(1)} %get-tuple-element.64), custom_call_target="InvertDiagBlocksLowerTriangular" | custom-call | tf_op jit(solution)/shard_map/jit(cholesky)/cholesky | solution.py:30
  382.6 1.3 convolution_subtract_fusion.17
  383.9 11.7 %cholesky.326 = f32[128,128]{1,0:T(8,128)S(1)} custom-call(f32[128,128]{1,0:T(8,128)S(1)} %cholesky.435), custom_call_target="Cholesky" | custom-call | tf_op jit(solution)/shard_map/jit(cholesky)/cholesky | solution.py:30
  395.7 9.8 %custom-call.31 = f32[1,128,128]{1,2,0:T(8,128)S(1)} custom-call(f32[1,128,128]{2,1,0:T(8,128)S(1)} %get-tuple-element.61), custom_call_target="InvertDiagBlocksLowerTriangular" | custom-call | tf_op jit(solution)/shard_map/jit(cholesky)/cholesky | solution.py:30
  405.7 1.2 convolution_subtract_fusion.19
  406.9 11.9 %cholesky.343 = f32[128,128]{1,0:T(8,128)S(1)} custom-call(f32[128,128]{1,0:T(8,128)S(1)} %convolution_subtract_fusion.19), custom_call_target="Cholesky" | custom-call | tf_op jit(solution)/shard_map/jit(cholesky)/cholesky | solution.py:30
  425.5 11.8 %while.4 = (s32[]{:T(128)}, f32[512,512]{1,0:T(8,128)}, s32[4,2]{0,1:T(2,128)S(1)}, f32[4,128,128]{2,1,0:T(8,128)S(1)}, s32[]{:T(128)}) while((s32[]{:T(128)}, f32[512,512]{1,0:T(8,128)}, s32[4,2]{0,1:T(2,128)S(1)}, f32[4,128,128]{2,1,0:T(8,128)S(1)}, s32[]{:T(128)}) %tuple.58), condition=%wide.while_cond, body=%wide.while_body.sunk | while | flops 2 | bytes 131189 | solution.py:31
  426.2 2.3 bitcast_dynamic-update-slice_fusion.4
  429.1 2.3 bitcast_dynamic-update-slice_fusion.4
  432.1 2.3 bitcast_dynamic-update-slice_fusion.4
  435.1 2.2 bitcast_dynamic-update-slice_fusion.4
  437.3 39.3 %custom-call.32 = f32[4,128,128]{1,2,0:T(8,128)S(1)} custom-call(f32[4,128,128]{2,1,0:T(8,128)S(1)} %get-tuple-element.18), custom_call_target="InvertDiagBlocksLowerTriangular" | custom-call | tf_op jit(solution)/shard_map/jit(_cho_solve)/triangular_solve | solution.py:31
  476.6 26.8 %all-reduce.9.cloned.1.call-done = f32[512,512]{1,0:T(8,128)} async-done(((f32[512,512]{1,0:T(8,128)}), f32[512,512]{1,0:T(8,128)}) %all-reduce.9.cloned.1.call-update) | async-done | bytes 1048592 | tf_op jit(solution)/shard_map/psum | solution.py:49
  503.4 1.4 fusion.37
  504.8 1.4 convolution_subtract_fusion.9
  506.6 1.4 convolution_subtract_fusion.8
  508.4 1.6 convolution_subtract_fusion.13
  515.0 33.7 %all-gather.3.cloned.1.call-done = f32[512,2048]{1,0:T(8,128)} async-done(((f32[512,512]{1,0:T(8,128)}), f32[512,2048]{1,0:T(8,128)}) %all-gather.3.cloned.1.call-update) | async-done | bytes 4194320 | tf_op jit(solution)/shard_map/all_gather | solution.py:51
  548.8 16.9 %convolution_subtract_fusion.1 = f32[1024,2048]{1,0:T(8,128)S(1)} fusion(f32[1024,2048]{1,0:T(8,128)} %param.9, f32[512,1024]{1,0:T(8,128)} %copy-done.5, f32[512,2048]{1,0:T(8,128)} %all-gather.3.cloned.1.call-done), kind=kOutput, calls=%fused_computation.6 | convolution fusion | flops 12886999040 | bytes 23068672 | tf_op jit(solution)/shard_map/dot_general | solution.py:52
  565.7 3.4 copy-done.2
  569.1 17.2 %fusion.100 = f32[512,2048]{1,0:T(8,128)} fusion(f32[512,1024]{1,0:T(8,128)} %copy-done.3, f32[1024,2048]{1,0:T(8,128)S(1)} %convolution_subtract_fusion.1), kind=kOutput, calls=%fused_computation.188 | convolution fusion | flops 12884901888 | bytes 14680064 | tf_op jit(solution)/shard_map/dot_general | solution.py:22
  588.1 11.7 %cholesky.358 = f32[128,128]{1,0:T(8,128)S(1)} custom-call(f32[128,128]{1,0:T(8,128)S(1)} %cholesky.439), custom_call_target="Cholesky" | custom-call | tf_op jit(solution)/shard_map/jit(cholesky)/cholesky | solution.py:30
  599.9 9.8 %custom-call.33 = f32[1,128,128]{1,2,0:T(8,128)S(1)} custom-call(f32[1,128,128]{2,1,0:T(8,128)S(1)} %get-tuple-element.57), custom_call_target="InvertDiagBlocksLowerTriangular" | custom-call | tf_op jit(solution)/shard_map/jit(cholesky)/cholesky | solution.py:30
  609.8 1.2 constant_dynamic-update-slice_fusion.3
  611.1 1.3 convolution_subtract_fusion.14
  612.3 11.7 %cholesky.377 = f32[128,128]{1,0:T(8,128)S(1)} custom-call(f32[128,128]{1,0:T(8,128)S(1)} %cholesky.443), custom_call_target="Cholesky" | custom-call | tf_op jit(solution)/shard_map/jit(cholesky)/cholesky | solution.py:30
  624.1 10.0 %custom-call.34 = f32[1,128,128]{1,2,0:T(8,128)S(1)} custom-call(f32[1,128,128]{2,1,0:T(8,128)S(1)} %get-tuple-element.54), custom_call_target="InvertDiagBlocksLowerTriangular" | custom-call | tf_op jit(solution)/shard_map/jit(cholesky)/cholesky | solution.py:30
  634.4 1.3 convolution_subtract_fusion.16
  635.7 11.7 %cholesky.398 = f32[128,128]{1,0:T(8,128)S(1)} custom-call(f32[128,128]{1,0:T(8,128)S(1)} %cholesky.448), custom_call_target="Cholesky" | custom-call | tf_op jit(solution)/shard_map/jit(cholesky)/cholesky | solution.py:30
  647.4 9.8 %custom-call.35 = f32[1,128,128]{1,2,0:T(8,128)S(1)} custom-call(f32[1,128,128]{2,1,0:T(8,128)S(1)} %get-tuple-element.51), custom_call_target="InvertDiagBlocksLowerTriangular" | custom-call | tf_op jit(solution)/shard_map/jit(cholesky)/cholesky | solution.py:30
  658.7 11.7 %cholesky.415 = f32[128,128]{1,0:T(8,128)S(1)} custom-call(f32[128,128]{1,0:T(8,128)S(1)} %convolution_subtract_fusion.18), custom_call_target="Cholesky" | custom-call | tf_op jit(solution)/shard_map/jit(cholesky)/cholesky | solution.py:30
  676.2 8.1 while.5
  676.8 1.4 bitcast_dynamic-update-slice_fusion.5
  678.8 1.4 bitcast_dynamic-update-slice_fusion.5
  680.8 1.4 bitcast_dynamic-update-slice_fusion.5
  682.8 1.4 bitcast_dynamic-update-slice_fusion.5
  684.2 39.3 %custom-call.36 = f32[4,128,128]{1,2,0:T(8,128)S(1)} custom-call(f32[4,128,128]{2,1,0:T(8,128)S(1)} %get-tuple-element.19), custom_call_target="InvertDiagBlocksLowerTriangular" | custom-call | tf_op jit(solution)/shard_map/jit(_cho_solve)/triangular_solve | solution.py:31
  723.5 31.3 %all-reduce.11.cloned.1.call-done = f32[512,512]{1,0:T(8,128)} async-done(((f32[512,512]{1,0:T(8,128)}), f32[512,512]{1,0:T(8,128)}) %all-reduce.11.cloned.1.call-update) | async-done | bytes 1048592 | tf_op jit(solution)/shard_map/psum | solution.py:49
  754.9 1.5 fusion.34
  756.3 1.3 convolution_subtract_fusion.5
  764.2 34.2 %all-gather.5.cloned.1.call-done = f32[512,2048]{1,0:T(8,128)} async-done(((f32[512,512]{1,0:T(8,128)}), f32[512,2048]{1,0:T(8,128)}) %all-gather.5.cloned.1.call-update) | async-done | bytes 4194320 | tf_op jit(solution)/shard_map/all_gather | solution.py:51
  798.4 8.1 pad_maximum_fusion
  806.5 17.1 %convolution_subtract_fusion = f32[1024,2048]{1,0:T(8,128)} fusion(f32[1024,2048]{1,0:T(8,128)} %copy-done.2, f32[512,1024]{1,0:T(8,128)S(1)} %copy-done.4, f32[512,2048]{1,0:T(8,128)S(1)} %copy-done.6), kind=kOutput, calls=%fused_computation.5 | convolution fusion | flops 12886999040 | bytes 23068672 | tf_op jit(solution)/shard_map/dot_general | solution.py:52
  (120 shorter events, 30.7 us)
Async XLA Ops:
  7.2 143.5 %copy-start = (f32[1024,440]{0,1:T(8,128)S(1)}, f32[1024,440]{0,1:T(8,128)}, u32[]{:S(2)}) copy-start(f32[1024,440]{0,1:T(8,128)} %param.8) | copy-start | bytes 5406724
  7.2 143.5 %all-reduce.15.cloned.1.call-start = ((), (), s32[]{:S(2)}) async-start(), calls=%async_computation.9 | async-start | bytes 3604480 | tf_op jit(solution)/shard_map/psum | solution.py:11
  9.9 2.7 copy-start.12
  12.6 312.9 %all-reduce.13.cloned.1.call-start = ((), (), s32[]{:S(2)}) async-start(), calls=%async_computation.8 | async-start | bytes 4194304 | tf_op jit(solution)/shard_map/psum | solution.py:47
  161.9 13.4 %copy-start.5 = (f32[512,1024]{1,0:T(8,128)}, f32[512,1024]{1,0:T(8,128)S(1)}, u32[]{:S(2)}) copy-start(f32[512,1024]{1,0:T(8,128)S(1)} %cosine_multiply_fusion.1) | copy-start | bytes 6291460
  162.0 13.4 %copy-start.11 = (f32[440,512]{1,0:T(8,128)S(1)}, f32[440,512]{1,0:T(8,128)}, u32[]{:S(2)}) copy-start(f32[440,512]{1,0:T(8,128)} %get-tuple-element.41) | copy-start | bytes 2703364
  185.7 1.4 copy-start.3
  191.6 233.8 %reduce-scatter.3.cloned.1.call-start = ((), (), s32[]{:S(2)}) async-start(), calls=%async_computation.2 | async-start | bytes 5242880 | tf_op jit(solution)/shard_map/reduce_scatter | solution.py:48
  209.7 293.7 %all-reduce.9.cloned.1.call-start = ((), (), s32[]{:S(2)}) async-start(), calls=%async_computation.3 | async-start | bytes 2097152 | tf_op jit(solution)/shard_map/psum | solution.py:49
  335.4 1.0 copy-start.8
  425.4 123.4 %all-gather.3.cloned.1.call-start = ((), (), s32[]{:S(2)}) async-start(), calls=%async_computation.4 | async-start | bytes 5242880 | tf_op jit(solution)/shard_map/all_gather | solution.py:51
  437.3 69.3 %copy-start.7 = (f32[512,512]{1,0:T(8,128)S(1)}, f32[512,512]{1,0:T(8,128)}, u32[]{:S(2)}) copy-start(f32[512,512]{1,0:T(8,128)} %get-tuple-element.187) | copy-start | bytes 3145732
  514.6 161.5 %reduce-scatter.5.cloned.1.call-start = ((), (), s32[]{:S(2)}) async-start(), calls=%async_computation.5 | async-start | bytes 5242880 | tf_op jit(solution)/shard_map/reduce_scatter | solution.py:48
  565.7 3.4 copy-start.2
  586.3 168.6 %all-reduce.11.cloned.1.call-start = ((), (), s32[]{:S(2)}) async-start(), calls=%async_computation.6 | async-start | bytes 2097152 | tf_op jit(solution)/shard_map/psum | solution.py:49
  587.1 1.0 copy-start.9
  676.1 122.3 %all-gather.5.cloned.1.call-start = ((), (), s32[]{:S(2)}) async-start(), calls=%async_computation.7 | async-start | bytes 5242880 | tf_op jit(solution)/shard_map/all_gather | solution.py:51
  754.9 3.2 copy-start.10
  798.4 8.1 copy-start.4
  798.4 8.1 copy-start.6
  806.5 17.2 %copy-start.1 = (f32[1024,440]{0,1:T(8,128)S(1)}, f32[1024,440]{0,1:T(8,128)}, u32[]{:S(2)}) copy-start(f32[1024,440]{0,1:T(8,128)} %param.8) | copy-start | bytes 5406724
Sparse Core Ops, SparseCore 0:
  14.0 136.6 all-reduce.14
  191.7 133.7 all-reduce.12
  328.6 43.2 reduce-scatter.2
  425.5 77.8 all-reduce.8
  514.7 34.0 all-gather.2
  586.4 44.4 reduce-scatter.4
  676.2 78.6 all-reduce.10
  764.3 34.0 all-gather.4
where the time goes:
time: 841 us; the launch traced here: 831 us
  waiting for transfers between devices  338 us (40%)
  other arithmetic  259 us (31%)
  matrix products  138 us (16%)
  blocking collectives  42.1 us (5%)
  local copies, waits for them, and re-layouts  29.9 us (4%)
  between operations  23 us (3%)
    another operation x30, other arithmetic, solve_block(): jnp.linalg.cholesky(gram_sum + damping * jnp.eye(width, dtype=gram_sum.dt...  159 us
    psum x1, waiting for transfers between devices, per_device(): gram_sum = lax.psum(local_product(feats, feats), ('wide', 'narrow'))  115 us
    psum x1, waiting for transfers between devices, from_root(): return lax.psum(kept, axis)  96 us
    another operation x7, other arithmetic, solve_block(): return jax.scipy.linalg.cho_solve((factor, True), cross_sum)  82.2 us
    all_gather x2, waiting for transfers between devices, per_device(): weights = lax.all_gather(weight_share, 'narrow', axis=1, tiled=True)  68 us
    psum x2, waiting for transfers between devices, per_device(): cross_share = lax.psum(cross_share, 'wide')  58.2 us
    dot_general x4, matrix products, local_product(): jnp.dot(left.T, right, precision=lax.Precision.HIGHEST, preferred_element...  53.1 us
    psum x1, blocking collectives, from_root(): return lax.psum(kept, axis)  42.1 us
  transfers between devices with their start and end apart: 8, of which 6 were waited for; matrix products, arithmetic and copies ran while one was open for 36% of the time, Pallas kernels for 0%

commit v1 on v0

--- a/solution.py
+++ b/solution.py
@@ -4,6 +4,27 @@
 from jax.sharding import PartitionSpec as P
 
 STEPS = 2
+
+
+def laid_out(blocks, dim):
+    dims = list(blocks.shape[1:])
+    dims[dim] *= blocks.shape[0]
+    return jnp.moveaxis(blocks, 0, dim).reshape(dims)
+
+
+def grow_blocks(array, axis):
+    devices, index = (lax.axis_size(axis), lax.axis_index(axis))
+    parts, bit = (array[None], 1)
+    while bit < devices:
+        theirs = lax.ppermute(parts, axis, [(i, i ^ bit) for i in range(devices)])
+        low = index & bit == 0
+        parts = jnp.concatenate([jnp.where(low, parts, theirs), jnp.where(low, theirs, parts)])
+        bit *= 2
+    return parts
+
+
+def collect(value, axis, dim):
+    return laid_out(grow_blocks(value, axis), dim)
 
 
 def from_root(value, axis, source):
@@ -48,7 +69,7 @@
         cross_share = lax.psum_scatter(cross_local, "narrow", scatter_dimension=1, tiled=True)
         cross_share = lax.psum(cross_share, "wide")
         weight_share = solve_block(gram_sum, cross_share)
-        weights = lax.all_gather(weight_share, "narrow", axis=1, tiled=True)
+        weights = collect(weight_share, "narrow", 1)
         residual = residual - jnp.dot(
             feats, weights, precision=lax.Precision.HIGHEST, preferred_element_type=jnp.float32
         )

time: 841 us -> 916 us (1.089)
  waiting for transfers between devices: 338 us -> 367 us
  local copies, waits for them, and re-layouts: 29.9 us -> 49.2 us
  matrix products: 138 us -> 155 us
    ppermute x0 -> x4, waiting for transfers between devices: none -> 98.1 us  [grow_blocks(): theirs = lax.ppermute(parts, axis, [(i, i ^ bit) for i in range(devices)])]
    all_gather x2 -> x0, waiting for transfers between devices: 68 us -> none  [per_device(): weights = lax.all_gather(weight_share, 'narrow', axis=1, tiled=True)]
    dot_general x2, matrix products: 34 us -> 60.9 us  [per_device(): jnp.dot(feats, weights, precision=lax.Precision.HIGHEST, preferred_elemen...]
    dot_general x4, matrix products: 53.1 us -> 42.5 us  [local_product(): jnp.dot(left.T, right, precision=lax.Precision.HIGHEST, preferred_element...]
    transpose x0 -> x2, local copies, waits for them, and re-layouts: none -> 10.5 us  [laid_out(): return jnp.moveaxis(blocks, 0, dim).reshape(dims)]
    another operation x7 -> x5, other arithmetic: 82.2 us -> 80.1 us  [solve_block(): return jax.scipy.linalg.cho_solve((factor, True), cross_sum)]
  transfers between devices with their start and end apart: 8 -> 10, of which waited for: 6 -> 8; matrix products, arithmetic and copies ran while one was open for 36% -> 33% of each run, Pallas kernels for 0% -> 0%
where the time goes in v1:
time: 916 us; the launch traced here: 906 us
  waiting for transfers between devices  367 us (40%)
  other arithmetic  265 us (29%)
  matrix products  155 us (17%)
  local copies, waits for them, and re-layouts  49.2 us (5%)
  blocking collectives  42.1 us (5%)
  between operations  23.1 us (3%)
    another operation x30, other arithmetic, solve_block(): jnp.linalg.cholesky(gram_sum + damping * jnp.eye(width, dtype=gram_sum.dt...  159 us
    psum x1, waiting for transfers between devices, per_device(): gram_sum = lax.psum(local_product(feats, feats), ('wide', 'narrow'))  116 us
    ppermute x4, waiting for transfers between devices, grow_blocks(): theirs = lax.ppermute(parts, axis, [(i, i ^ bit) for i in range(devices)])  98.1 us
    psum x1, waiting for transfers between devices, from_root(): return lax.psum(kept, axis)  95.9 us
    another operation x5, other arithmetic, solve_block(): return jax.scipy.linalg.cho_solve((factor, True), cross_sum)  80.1 us
    dot_general x2, matrix products, per_device(): jnp.dot(feats, weights, precision=lax.Precision.HIGHEST, preferred_elemen...  60.9 us
    psum x2, waiting for transfers between devices, per_device(): cross_share = lax.psum(cross_share, 'wide')  57.6 us
    dot_general x4, matrix products, local_product(): jnp.dot(left.T, right, precision=lax.Precision.HIGHEST, preferred_element...  42.5 us
  transfers between devices with their start and end apart: 10, of which 8 were waited for; matrix products, arithmetic and copies ran while one was open for 33% of the time, Pallas kernels for 0%

profile of v1, /device:TPU:0, one launch (start us, length us, event | category | flops | bytes accessed | tf_op | source)
XLA Modules:
  0.0 905.7 jit_solution(2873277519777211152)
XLA Ops:
  7.2 1.4 fusion.96
  9.9 2.6 select_bitcast_fusion
  12.6 42.1 %all-reduce.1 = (f32[512]{0:T(512)S(1)}, f32[512]{0:T(512)S(1)}) all-reduce(f32[512]{0:T(512)S(1)} %bitcast.163, f32[512]{0:T(512)S(1)} %bitcast.162), channel_id=1, replica_groups=mesh['wide'=8,'narrow'=4] {'wide','narrow'}, use_global_device_ids=true, to_apply=%region_1.2 | all-reduce | flops 1024 | bytes 8192 | tf_op jit(solution)/shard_map/psum | solution.py:32
  54.8 95.9 %all-reduce.15.cloned.1.call-done = (f32[440,512]{1,0:T(8,128)}, f32[440,512]{1,0:T(8,128)}) async-done(((f32[440,512]{1,0:T(8,128)}, f32[440,512]{1,0:T(8,128)}), (f32[440,512]{1,0:T(8,128)}, f32[440,512]{1,0:T(8,128)})) %all-reduce.15.cloned.1.call-update) | async-done | bytes 1802256 | tf_op jit(solution)/shard_map/psum | solution.py:32
  150.7 11.2 %cosine_multiply_fusion.1 = f32[512,1024]{1,0:T(8,128)S(1)} fusion(f32[440,512]{1,0:T(8,128)} %get-tuple-element.42, f32[1024,440]{0,1:T(8,128)S(1)} %copy-done, f32[512]{0:T(512)S(1)} %get-tuple-element.38), kind=kOutput, calls=%fused_computation.12 | convolution fusion | flops 2769289216 | bytes 4802560 | tf_op jit(solution)/shard_map/dot_general | solution.py:36
  162.0 4.8 fusion.97
  166.8 10.5 %cosine_multiply_fusion = f32[512,1024]{1,0:T(8,128)S(1)} fusion(f32[440,512]{1,0:T(8,128)S(1)} %copy-done.14, f32[1024,440]{0,1:T(8,128)S(1)} %copy-done, f32[512]{0:T(512)S(1)} %get-tuple-element.39), kind=kOutput, calls=%fused_computation.11 | convolution fusion | flops 2769289216 | bytes 4802560 | tf_op jit(solution)/shard_map/dot_general | solution.py:36
  177.3 1.4 copy-done.3
  178.7 4.5 fusion.99
  183.3 18.0 %fusion.98 = f32[512,2048]{1,0:T(8,128)} fusion(f32[512,1024]{1,0:T(8,128)} %copy-done.5, f32[1024,2048]{1,0:T(8,128)} %param.9), kind=kOutput, calls=%fused_computation.198 | convolution fusion | flops 12884901888 | bytes 14680064 | tf_op jit(solution)/shard_map/dot_general | solution.py:43
  201.5 115.6 %all-reduce.13.cloned.1.call-done = (f32[512,512]{0,1:T(8,128)}, f32[512,512]{0,1:T(8,128)}) async-done(((f32[512,512]{0,1:T(8,128)}, f32[512,512]{0,1:T(8,128)}), (f32[512,512]{0,1:T(8,128)}, f32[512,512]{0,1:T(8,128)})) %all-reduce.13.cloned.1.call-update) | async-done | bytes 2097168 | tf_op jit(solution)/shard_map/psum | solution.py:68
  317.1 2.0 select_reduce_fusion
  319.7 2.0 select_reduce_fusion.1
  322.3 1.8 select_add_fusion
  325.5 1.5 fusion.1
  328.0 11.7 %cholesky.286 = f32[128,128]{1,0:T(8,128)S(1)} custom-call(f32[128,128]{1,0:T(8,128)S(1)} %cholesky.426), custom_call_target="Cholesky" | custom-call | tf_op jit(solution)/shard_map/jit(cholesky)/cholesky | solution.py:51
  339.8 9.8 %custom-call.29 = f32[1,128,128]{1,2,0:T(8,128)S(1)} custom-call(f32[1,128,128]{2,1,0:T(8,128)S(1)} %get-tuple-element.77), custom_call_target="InvertDiagBlocksLowerTriangular" | custom-call | tf_op jit(solution)/shard_map/jit(cholesky)/cholesky | solution.py:51
  352.2 11.7 %cholesky.305 = f32[128,128]{1,0:T(8,128)S(1)} custom-call(f32[128,128]{1,0:T(8,128)S(1)} %cholesky.430), custom_call_target="Cholesky" | custom-call | tf_op jit(solution)/shard_map/jit(cholesky)/cholesky | solution.py:51
  364.0 10.0 %custom-call.30 = f32[1,128,128]{1,2,0:T(8,128)S(1)} custom-call(f32[1,128,128]{2,1,0:T(8,128)S(1)} %get-tuple-element.74), custom_call_target="InvertDiagBlocksLowerTriangular" | custom-call | tf_op jit(solution)/shard_map/jit(cholesky)/cholesky | solution.py:51
  375.5 11.7 %cholesky.326 = f32[128,128]{1,0:T(8,128)S(1)} custom-call(f32[128,128]{1,0:T(8,128)S(1)} %cholesky.435), custom_call_target="Cholesky" | custom-call | tf_op jit(solution)/shard_map/jit(cholesky)/cholesky | solution.py:51
  387.3 9.8 %custom-call.31 = f32[1,128,128]{1,2,0:T(8,128)S(1)} custom-call(f32[1,128,128]{2,1,0:T(8,128)S(1)} %get-tuple-element.71), custom_call_target="InvertDiagBlocksLowerTriangular" | custom-call | tf_op jit(solution)/shard_map/jit(cholesky)/cholesky | solution.py:51
  398.6 12.1 %cholesky.343 = f32[128,128]{1,0:T(8,128)S(1)} custom-call(f32[128,128]{1,0:T(8,128)S(1)} %convolution_subtract_fusion.19), custom_call_target="Cholesky" | custom-call | tf_op jit(solution)/shard_map/jit(cholesky)/cholesky | solution.py:51
  417.3 11.8 %while.4 = (s32[]{:T(128)}, f32[512,512]{1,0:T(8,128)}, s32[4,2]{0,1:T(2,128)S(1)}, f32[4,128,128]{2,1,0:T(8,128)S(1)}, s32[]{:T(128)}) while((s32[]{:T(128)}, f32[512,512]{1,0:T(8,128)}, s32[4,2]{0,1:T(2,128)S(1)}, f32[4,128,128]{2,1,0:T(8,128)S(1)}, s32[]{:T(128)}) %tuple.63), condition=%wide.while_cond, body=%wide.while_body.sunk | while | flops 2 | bytes 131189 | solution.py:52
  418.0 2.3 bitcast_dynamic-update-slice_fusion.4
  421.0 2.3 bitcast_dynamic-update-slice_fusion.4
  423.9 2.3 bitcast_dynamic-update-slice_fusion.4
  426.9 2.2 bitcast_dynamic-update-slice_fusion.4
  429.1 39.3 %custom-call.32 = f32[4,128,128]{1,2,0:T(8,128)S(1)} custom-call(f32[4,128,128]{2,1,0:T(8,128)S(1)} %get-tuple-element.18), custom_call_target="InvertDiagBlocksLowerTriangular" | custom-call | tf_op jit(solution)/shard_map/jit(_cho_solve)/triangular_solve | solution.py:52
  468.5 26.6 %all-reduce.9.cloned.1.call-done = f32[512,512]{1,0:T(8,128)} async-done(((f32[512,512]{1,0:T(8,128)}), f32[512,512]{1,0:T(8,128)}) %all-reduce.9.cloned.1.call-update) | async-done | bytes 1048592 | tf_op jit(solution)/shard_map/psum | solution.py:70
  500.1 1.6 convolution_subtract_fusion.13
  506.2 2.8 collective-permute-done
  508.9 1.4 broadcast_select_fusion.7
  510.4 1.6 pad_maximum_fusion.1
  512.0 1.5 collective-permute-start.1
  513.5 46.5 %collective-permute-done.1 = f32[2,512,512]{2,1,0:T(8,128)} collective-permute-done((f32[2,512,512]{2,1,0:T(8,128)}, f32[2,512,512]{2,1,0:T(8,128)}, u32[]{:S(2)}, u32[]{:S(2)}) %collective-permute-start.1) | collective-permute-done | bytes 2097184 | tf_op jit(solution)/shard_map/ppermute | solution.py:19
  560.0 2.4 broadcast_select_fusion.3
  562.4 2.5 maximum_bitcast_fusion
  564.9 5.2 copy.13
  570.2 29.9 %convolution_subtract_fusion.1 = f32[1024,2048]{1,0:T(8,128)S(1)} fusion(f32[1024,2048]{1,0:T(8,128)} %param.9, f32[512,1024]{1,0:T(8,128)} %copy-done.5, f32[512,2048]{0,1:T(8,128)} %bitcast.158), kind=kOutput, calls=%fused_computation.8 | convolution fusion | flops 12886999040 | bytes 23068672 | tf_op jit(solution)/shard_map/dot_general | solution.py:73
  600.1 3.4 copy-done.2
  603.5 15.2 %fusion.100 = f32[512,2048]{1,0:T(8,128)} fusion(f32[512,1024]{1,0:T(8,128)S(1)} %copy-done.4, f32[1024,2048]{1,0:T(8,128)S(1)} %convolution_subtract_fusion.1), kind=kOutput, calls=%fused_computation.200 | convolution fusion | flops 12884901888 | bytes 14680064 | tf_op jit(solution)/shard_map/dot_general | solution.py:43
  620.7 11.7 %cholesky.358 = f32[128,128]{1,0:T(8,128)S(1)} custom-call(f32[128,128]{1,0:T(8,128)S(1)} %cholesky.439), custom_call_target="Cholesky" | custom-call | tf_op jit(solution)/shard_map/jit(cholesky)/cholesky | solution.py:51
  632.4 9.8 %custom-call.33 = f32[1,128,128]{1,2,0:T(8,128)S(1)} custom-call(f32[1,128,128]{2,1,0:T(8,128)S(1)} %get-tuple-element.67), custom_call_target="InvertDiagBlocksLowerTriangular" | custom-call | tf_op jit(solution)/shard_map/jit(cholesky)/cholesky | solution.py:51
  644.9 11.7 %cholesky.377 = f32[128,128]{1,0:T(8,128)S(1)} custom-call(f32[128,128]{1,0:T(8,128)S(1)} %cholesky.443), custom_call_target="Cholesky" | custom-call | tf_op jit(solution)/shard_map/jit(cholesky)/cholesky | solution.py:51
  656.7 9.9 %custom-call.34 = f32[1,128,128]{1,2,0:T(8,128)S(1)} custom-call(f32[1,128,128]{2,1,0:T(8,128)S(1)} %get-tuple-element.64), custom_call_target="InvertDiagBlocksLowerTriangular" | custom-call | tf_op jit(solution)/shard_map/jit(cholesky)/cholesky | solution.py:51
  668.2 11.7 %cholesky.398 = f32[128,128]{1,0:T(8,128)S(1)} custom-call(f32[128,128]{1,0:T(8,128)S(1)} %cholesky.448), custom_call_target="Cholesky" | custom-call | tf_op jit(solution)/shard_map/jit(cholesky)/cholesky | solution.py:51
  679.9 9.8 %custom-call.35 = f32[1,128,128]{1,2,0:T(8,128)S(1)} custom-call(f32[1,128,128]{2,1,0:T(8,128)S(1)} %get-tuple-element.61), custom_call_target="InvertDiagBlocksLowerTriangular" | custom-call | tf_op jit(solution)/shard_map/jit(cholesky)/cholesky | solution.py:51
  691.2 11.7 %cholesky.415 = f32[128,128]{1,0:T(8,128)S(1)} custom-call(f32[128,128]{1,0:T(8,128)S(1)} %convolution_subtract_fusion.18), custom_call_target="Cholesky" | custom-call | tf_op jit(solution)/shard_map/jit(cholesky)/cholesky | solution.py:51
  708.6 8.1 while.5
  709.2 1.4 bitcast_dynamic-update-slice_fusion.5
  711.3 1.4 bitcast_dynamic-update-slice_fusion.5
  713.3 1.4 bitcast_dynamic-update-slice_fusion.5
  715.3 1.4 bitcast_dynamic-update-slice_fusion.5
  716.7 39.3 %custom-call.36 = f32[4,128,128]{1,2,0:T(8,128)S(1)} custom-call(f32[4,128,128]{2,1,0:T(8,128)S(1)} %get-tuple-element.19), custom_call_target="InvertDiagBlocksLowerTriangular" | custom-call | tf_op jit(solution)/shard_map/jit(_cho_solve)/triangular_solve | solution.py:52
  756.0 31.0 %all-reduce.11.cloned.1.call-done = f32[512,512]{1,0:T(8,128)} async-done(((f32[512,512]{1,0:T(8,128)}), f32[512,512]{1,0:T(8,128)}) %all-reduce.11.cloned.1.call-update) | async-done | bytes 1048592 | tf_op jit(solution)/shard_map/psum | solution.py:70
  787.0 1.5 fusion.34
  795.3 2.6 collective-permute-done.2
  798.4 1.5 collective-permute-start.3
  800.0 46.2 %collective-permute-done.3 = f32[2,512,512]{2,1,0:T(8,128)S(1)} collective-permute-done((f32[2,512,512]{2,1,0:T(8,128)S(1)}, f32[2,512,512]{2,1,0:T(8,128)S(1)}, u32[]{:S(2)}, u32[]{:S(2)}) %collective-permute-start.3) | collective-permute-done | bytes 2097184 | tf_op jit(solution)/shard_map/ppermute | solution.py:19
  846.7 2.5 maximum_bitcast_fusion.1
  849.2 5.2 copy.16
  854.4 31.0 %convolution_subtract_fusion = f32[1024,2048]{1,0:T(8,128)} fusion(f32[1024,2048]{1,0:T(8,128)} %copy-done.2, f32[512,1024]{1,0:T(8,128)} %copy-done.3, f32[512,2048]{0,1:T(8,128)} %bitcast.160), kind=kOutput, calls=%fused_computation.7 | convolution fusion | flops 12886999040 | bytes 23068672 | tf_op jit(solution)/shard_map/dot_general | solution.py:73
  885.5 4.2 pad_maximum_fusion
  889.7 8.8 copy.19
  (139 shorter events, 45.7 us)
Async XLA Ops:
  7.2 143.5 %copy-start = (f32[1024,440]{0,1:T(8,128)S(1)}, f32[1024,440]{0,1:T(8,128)}, u32[]{:S(2)}) copy-start(f32[1024,440]{0,1:T(8,128)} %param.8) | copy-start | bytes 5406724
  7.2 143.5 %all-reduce.15.cloned.1.call-start = ((), (), s32[]{:S(2)}) async-start(), calls=%async_computation.7 | async-start | bytes 3604480 | tf_op jit(solution)/shard_map/psum | solution.py:32
  9.9 2.7 copy-start.15
  12.6 304.5 %all-reduce.13.cloned.1.call-start = ((), (), s32[]{:S(2)}) async-start(), calls=%async_computation.6 | async-start | bytes 4194304 | tf_op jit(solution)/shard_map/psum | solution.py:68
  161.9 4.8 copy-start.5
  162.0 4.8 copy-start.14
  177.3 1.4 copy-start.3
  183.2 234.0 %reduce-scatter.3.cloned.1.call-start = ((), (), s32[]{:S(2)}) async-start(), calls=%async_computation.2 | async-start | bytes 5242880 | tf_op jit(solution)/shard_map/reduce_scatter | solution.py:69
  201.3 293.8 %all-reduce.9.cloned.1.call-start = ((), (), s32[]{:S(2)}) async-start(), calls=%async_computation.3 | async-start | bytes 2097152 | tf_op jit(solution)/shard_map/psum | solution.py:70
  327.0 1.0 copy-start.10
  417.2 291.3 %reduce-scatter.5.cloned.1.call-start = ((), (), s32[]{:S(2)}) async-start(), calls=%async_computation.4 | async-start | bytes 5242880 | tf_op jit(solution)/shard_map/reduce_scatter | solution.py:69
  429.1 69.1 %copy-start.9 = (f32[512,512]{1,0:T(8,128)S(1)}, f32[512,512]{1,0:T(8,128)}, u32[]{:S(2)}) copy-start(f32[512,512]{1,0:T(8,128)} %get-tuple-element.192) | copy-start | bytes 3145732
  468.4 35.3 %copy-start.12 = (f32[4,128,128]{1,2,0:T(8,128)}, f32[4,128,128]{1,2,0:T(8,128)S(1)}, u32[]{:S(2)}) copy-start(f32[4,128,128]{1,2,0:T(8,128)S(1)} %custom-call.32) | copy-start | bytes 786436
  506.1 2.9 collective-permute-start
  510.4 1.6 copy-start.8
  512.0 48.0 %collective-permute-start.1 = (f32[2,512,512]{2,1,0:T(8,128)}, f32[2,512,512]{2,1,0:T(8,128)}, u32[]{:S(2)}, u32[]{:S(2)}) collective-permute-start(f32[2,512,512]{2,1,0:T(8,128)} %pad_maximum_fusion.1), channel_id=1, source_target_pairs={{0,2},{1,3},{2,0},{3,1},{4,6},{5,7},{6,4},{7,5},{8,10},{9,11},{10,... | collective-permute-start | bytes 6291464 | tf_op jit(solution)/shard_map/ppermute | solution.py:19
  570.2 33.3 %copy-start.4 = (f32[512,1024]{1,0:T(8,128)S(1)}, f32[512,1024]{1,0:T(8,128)}, u32[]{:S(2)}) copy-start(f32[512,1024]{1,0:T(8,128)} %copy-done.3) | copy-start | bytes 6291460
  600.1 3.4 copy-start.2
  618.6 168.3 %all-reduce.11.cloned.1.call-start = ((), (), s32[]{:S(2)}) async-start(), calls=%async_computation.5 | async-start | bytes 2097152 | tf_op jit(solution)/shard_map/psum | solution.py:70
  619.7 1.0 copy-start.11
  787.0 3.2 copy-start.13
  795.3 2.7 collective-permute-start.2
  798.4 47.7 %collective-permute-start.3 = (f32[2,512,512]{2,1,0:T(8,128)S(1)}, f32[2,512,512]{2,1,0:T(8,128)S(1)}, u32[]{:S(2)}, u32[]{:S(2)}) collective-permute-start(f32[2,512,512]{2,1,0:T(8,128)S(1)} %pad_maximum_fusion.2), channel_id=1, source_target_pairs={{0,2},{1,3},{2,0},{3,1},{4,6},{5,7},{6,4},{7,5},{8,10},{9,11},{10,... | collective-permute-start | bytes 6291464 | tf_op jit(solution)/shard_map/ppermute | solution.py:19
  854.4 31.0 %copy-start.6 = (f32[512,4,512]{0,2,1:T(8,128)S(1)}, f32[512,4,512]{0,2,1:T(8,128)}, u32[]{:S(2)}) copy-start(f32[512,4,512]{0,2,1:T(8,128)} %copy.13) | copy-start | bytes 12582916
  854.4 31.0 %copy-start.7 = (f32[512,4,512]{0,2,1:T(8,128)S(1)}, f32[512,4,512]{0,2,1:T(8,128)}, u32[]{:S(2)}) copy-start(f32[512,4,512]{0,2,1:T(8,128)} %copy.16) | copy-start | bytes 12582916
  889.7 8.8 copy-start.1
Sparse Core Ops, SparseCore 0:
  14.0 136.6 all-reduce.14
  183.4 133.7 all-reduce.12
  320.2 43.2 reduce-scatter.2
  417.4 77.6 all-reduce.8
  618.8 44.1 reduce-scatter.4
  708.7 78.2 all-reduce.10
